TPU v7x, 256 devices: a whole 4x4x8 slice. The times are simulated.
256 devices in a mesh: tm: 16 (over y, x), space: 2 (over core), head: 8 (over z).
Axes of the slice: x: 4, y: 4, z: 8, core: 2. Of those that a mesh axis runs over, the one named last changes fastest.
Arguments:
- query: bfloat16 [16, 8, 80, 5120], P('tm', 'space', None, 'head'), may hold values from -5 to 5
- key: bfloat16 [16, 8, 80, 5120], P('tm', 'space', None, 'head'), may hold values from -5 to 5
- value: bfloat16 [16, 8, 80, 5120], P('tm', 'space', None, 'head'), may hold values from -6 to 6
- window: int32 [16, 16], replicated, may hold values from -1 to 4, as said below
- out_weight: bfloat16 [5120, 5120], P('head'), may hold values from -0.078125 to 0.078125
Outputs:
- projected: bfloat16 [16, 8, 80, 5120], P('tm', 'space', None, 'head')
Inputs may be any that keep to these rules, and one draw needn't show every extreme that they name: window[f, f] = 4 for every frame f.
All inputs are finite; a program needn't handle non-finite values.
Results may differ from a plain program's by a relative error of at most 0.023.
Values may be sent and summed in bfloat16 or wider, within the bound.
A program may use at most 128 MiB of HBM per device.

v0:
```python
import math
import jax
import jax.numpy as jnp
from jax import lax
from jax.sharding import PartitionSpec as P

HD = 128
HALO = 4
NEG_FILL = -1e30


def padded_2(x, sides, width):
    for axis, dim in sides:
        size, length = (lax.axis_size(axis), x.shape[dim])
        up = [(i, (i + 1) % size) for i in range(size - 1)]
        down = [(j, i) for i, j in up]
        last = lax.slice_in_dim(x, length - width, length, axis=dim)
        first = lax.slice_in_dim(x, 0, width, axis=dim)
        before = lax.ppermute(last, axis, up)
        after = lax.ppermute(first, axis, down)
        x = jnp.concatenate([before, x, after], axis=dim)
    return x


def frame_mask(widths, query_rows, key_rows, total_rows, width):
    count = widths.shape[0]
    distance = jnp.abs(query_rows[:, None] - key_rows[None, :])
    inside_grid = (key_rows >= 0) & (key_rows < total_rows)
    inside = (
        (widths[:, None, None] >= 0)
        & (distance[None] <= widths[:, None, None])
        & inside_grid[None, None, :]
    )
    span_rows = key_rows.shape[0]
    full = jnp.broadcast_to(
        inside[:, :, None, :, None], (count, query_rows.shape[0], width, span_rows, width)
    )
    return full.reshape(count * query_rows.shape[0] * width, span_rows * width)


def absorb(state, queries, keys, values, mask):
    run_max, run_sum, run_acc = state
    scale = 1.0 / math.sqrt(HD)
    scores = jnp.einsum("qhd,khd->hqk", queries, keys, preferred_element_type=jnp.float32) * scale
    new_max = jnp.maximum(run_max, jnp.max(jnp.where(mask[None], scores, NEG_FILL), axis=-1))
    weights = jnp.where(mask[None], jnp.exp(scores - new_max[..., None]), 0.0)
    factor = jnp.exp(run_max - new_max)
    new_sum = run_sum * factor + jnp.sum(weights, axis=-1)
    new_acc = run_acc * factor[..., None] + jnp.einsum(
        "hqk,khd->hqd", weights.astype(jnp.bfloat16), values, preferred_element_type=jnp.float32
    )
    return (new_max, new_sum, new_acc)


def absorb_frame(state, queries, widths, kv_frame, query_rows, key_rows, total_rows):
    span_rows, width, feats = (kv_frame.shape[1], kv_frame.shape[2], kv_frame.shape[3])
    heads_dev = feats // HD
    keys = kv_frame[0].reshape(span_rows * width, heads_dev, HD)
    values = kv_frame[1].reshape(span_rows * width, heads_dev, HD)
    mask = frame_mask(widths, query_rows, key_rows, total_rows, width)
    return absorb(state, queries, keys, values, mask)


def empty_state(heads_dev, count):
    return (
        jnp.full((heads_dev, count), NEG_FILL, jnp.float32),
        jnp.zeros((heads_dev, count), jnp.float32),
        jnp.zeros((heads_dev, count, HD), jnp.float32),
    )


def body(query, key, value, window, out_weight):
    frames_dev, rows_dev, width, feats = query.shape
    heads_dev = feats // HD
    qcount = frames_dev * rows_dev * width
    total_rows = rows_dev * lax.axis_size("space")
    first_row = lax.axis_index("space") * rows_dev
    first_frame = lax.axis_index("tm") * frames_dev
    query_rows = first_row + jnp.arange(rows_dev, dtype=jnp.int32)
    stacked = jnp.stack([key, value])
    padded = padded_2(stacked, (("space", 2),), HALO)
    key_rows = first_row - HALO + jnp.arange(rows_dev + 2 * HALO, dtype=jnp.int32)
    my_windows = lax.dynamic_slice_in_dim(window, first_frame, frames_dev, 0)
    queries = query.reshape(qcount, heads_dev, HD)
    piece = lax.all_gather(padded, "tm", axis=1, tiled=True)

    def one_frame(carry, offset):
        kv_frame = lax.dynamic_index_in_dim(piece, offset, 1, False)
        widths = lax.dynamic_index_in_dim(my_windows, offset, 1, False)
        return (
            absorb_frame(carry, queries, widths, kv_frame, query_rows, key_rows, total_rows),
            None,
        )

    result, unused = lax.scan(
        one_frame, empty_state(heads_dev, qcount), jnp.arange(piece.shape[1], dtype=jnp.int32)
    )
    run_max, run_sum, run_acc = result
    attended = (
        (run_acc / run_sum[..., None])
        .transpose(1, 0, 2)
        .reshape(qcount, feats)
        .astype(jnp.bfloat16)
    )
    share_rows = out_weight.shape[1] // lax.axis_size("head")
    mixed = lax.psum_scatter(
        lax.dot_general(
            out_weight, attended, (((0,), (1,)), ((), ())), preferred_element_type=jnp.float32
        ).astype(jnp.bfloat16),
        "head",
        scatter_dimension=0,
        tiled=True,
    ).astype(jnp.float32)
    return mixed.T.reshape(frames_dev, rows_dev, width, share_rows).astype(jnp.bfloat16)


def solution(mesh):
    placed = (
        P("tm", "space", None, "head"),
        P("tm", "space", None, "head"),
        P("tm", "space", None, "head"),
        P(),
        P("head", None),
    )
    return jax.shard_map(
        body, mesh=mesh, in_specs=placed, out_specs=P("tm", "space", None, "head"), check_vma=False
    )
```

profile of v0, /device:TPU:1, one launch (start us, length us, event | category | flops | bytes accessed | tf_op | source)
XLA Modules:
  0.0 810.0 jit_solution(69779024183798448)
XLA Ops:
  9.1 5.2 collective-permute-start.1
  16.2 2.9 pad_maximum_fusion
  21.1 230.9 %all-gather.2.cloned.1.call-done = bf16[2,16,12,80,640]{4,3,2,1,0:T(8,128)(2,1)} async-done(((bf16[2,1,12,80,640]{4,3,2,1,0:T(8,128)(2,1)}), bf16[2,16,12,80,640]{4,3,2,1,0:T(8,128)(2,1)}) %all-gather.2.cloned.1.call-update) | async-done | bytes 39321616 | tf_op jit(solution)/shard_map/all_gather | solution.py:85
  252.0 484.5 %while.15 = (s32[]{:T(128)}, f32[5,320]{1,0:T(8,128)S(1)}, f32[5,320]{1,0:T(8,128)}, f32[5,320,128]{2,1,0:T(8,128)}, s32[16]{0:T(128)S(1)}, /*index=5*/s32[1,16]...) while((s32[]{:T(128)}, f32[5,320]{1,0:T(8,128)S(1)}, ...), condition=%wide.region_3.4_spmd.clone, body=%wide.region_0.3_spmd.clone.sunk | while | flops 803950720 | bytes 35329148 | solution.py:95
  260.6 2.6 squeeze.19
  263.2 5.7 fusion.43
  269.0 4.9 fusion.44
  275.9 5.5 fusion.46
  292.7 5.7 fusion.43
  298.5 4.9 fusion.44
  306.1 5.7 fusion.46
  320.4 2.6 squeeze.19
  323.1 5.7 fusion.43
  328.8 4.9 fusion.44
  336.5 5.7 fusion.46
  350.7 2.6 squeeze.19
  353.4 5.7 fusion.43
  359.1 4.9 fusion.44
  366.8 5.7 fusion.46
  381.1 2.6 squeeze.19
  383.7 5.7 fusion.43
  389.5 4.9 fusion.44
  397.1 5.7 fusion.46
  411.4 2.6 squeeze.19
  414.1 5.7 fusion.43
  419.8 4.9 fusion.44
  427.4 5.7 fusion.46
  444.4 5.7 fusion.43
  450.1 4.9 fusion.44
  457.8 5.7 fusion.46
  472.1 2.6 squeeze.19
  474.7 5.7 fusion.43
  480.5 4.9 fusion.44
  488.1 5.7 fusion.46
  505.1 5.7 fusion.43
  510.8 4.9 fusion.44
  518.4 5.7 fusion.46
  532.7 2.6 squeeze.19
  535.4 5.7 fusion.43
  541.1 4.9 fusion.44
  548.8 5.7 fusion.46
  563.1 2.6 squeeze.19
  565.7 5.7 fusion.43
  571.4 4.9 fusion.44
  579.1 5.7 fusion.46
  593.4 2.6 squeeze.19
  596.0 5.7 fusion.43
  601.8 4.9 fusion.44
  609.4 5.7 fusion.46
  626.4 5.7 fusion.43
  632.1 4.9 fusion.44
  639.8 5.7 fusion.46
  656.7 5.7 fusion.43
  662.4 4.9 fusion.44
  670.1 5.7 fusion.46
  687.0 5.7 fusion.43
  692.8 4.9 fusion.44
  700.4 5.7 fusion.46
  717.4 5.7 fusion.43
  723.1 4.9 fusion.44
  730.8 5.7 fusion.46
  738.9 5.8 fusion.23
  744.7 3.6 copy.22
  748.3 52.9 %reduce-scatter.4.cloned.1.call-done = bf16[640,320]{1,0:T(8,128)(2,1)} async-done(((bf16[5120,320]{1,0:T(8,128)(2,1)}), bf16[640,320]{1,0:T(8,128)(2,1)}) %reduce-scatter.4.cloned.1.call-update) | async-done | bytes 409616
  (335 shorter events, 180.5 us)
Async XLA Ops:
  6.5 14.0 %copy-start = (s32[16,16]{1,0:T(8,128)S(1)}, s32[16,16]{1,0:T(8,128)}, u32[]{:S(2)}) copy-start(s32[16,16]{1,0:T(8,128)} %param.10) | copy-start | bytes 3076
  6.5 12.7 %copy-start.2 = (bf16[1,4,80,640]{3,2,1,0:T(8,128)(2,1)S(1)}, bf16[1,4,80,640]{3,2,1,0:T(8,128)(2,1)}, u32[]{:S(2)}) copy-start(bf16[1,4,80,640]{3,2,1,0:T(8,128)(2,1)} %param.7) | copy-start | bytes 1228804
  6.5 245.4 %all-gather.2.cloned.1.call-start = ((), (), s32[]{:S(2)}) async-start(), calls=%async_computation.1 | async-start | bytes 41779200 | tf_op jit(solution)/shard_map/all_gather | solution.py:85
  7.8 6.5 collective-permute-start
  9.1 7.1 collective-permute-start.1
  19.1 782.1 %reduce-scatter.4.cloned.1.call-start = ((), (), s32[]{:S(2)}) async-start(), calls=%async_computation.2 | async-start | bytes 4423680
  252.0 3.7 copy-start.3
  275.9 5.5 copy-start.4
  281.4 3.7 copy-start.3
  306.1 5.7 copy-start.4
  311.8 3.7 copy-start.3
  336.4 5.7 copy-start.4
  342.1 3.7 copy-start.3
  366.8 5.7 copy-start.4
  372.4 3.7 copy-start.3
  397.1 5.7 copy-start.4
  402.8 3.7 copy-start.3
  427.4 5.7 copy-start.4
  433.1 3.7 copy-start.3
  457.8 5.7 copy-start.4
  463.4 3.7 copy-start.3
  488.1 5.7 copy-start.4
  493.8 3.7 copy-start.3
  518.4 5.7 copy-start.4
  524.1 3.7 copy-start.3
  548.8 5.7 copy-start.4
  554.4 3.7 copy-start.3
  579.1 5.7 copy-start.4
  584.8 3.7 copy-start.3
  609.4 5.7 copy-start.4
  615.1 3.7 copy-start.3
  639.8 5.7 copy-start.4
  645.4 3.7 copy-start.3
  670.1 5.7 copy-start.4
  675.8 3.7 copy-start.3
  700.4 5.7 copy-start.4
  706.1 3.7 copy-start.3
  730.8 5.7 copy-start.4
  738.9 64.3 %copy-start.1 = (s32[16,16]{1,0:T(8,128)S(1)}, s32[16,16]{1,0:T(8,128)}, u32[]{:S(2)}) copy-start(s32[16,16]{1,0:T(8,128)} %param.10) | copy-start | bytes 3076
Sparse Core Ops, SparseCore 0:
  19.2 232.7 all-gather.1
  748.4 52.6 reduce-scatter.3
where the time goes:
time: 813 us; the launch traced here: 810 us
  waiting for transfers between devices  286 us (35%)
  matrix products  188 us (23%)
  other arithmetic  145 us (18%)
  local copies, waits for them, and re-layouts  141 us (17%)
  loops' own time  30.9 us (4%)
  between operations  13.5 us (2%)
    all_gather x1, waiting for transfers between devices, body(): piece = lax.all_gather(padded, 'tm', axis=1, tiled=True)  231 us
    dot_general x16, matrix products, absorb(): jnp.einsum('qhd,khd->hqk', queries, keys, preferred_element_type=jnp.floa...  91.6 us
    dot_general x16, matrix products, absorb(): jnp.einsum('hqk,khd->hqd', weights.astype(jnp.bfloat16), values, preferre...  90.3 us
    reduce_sum x16, other arithmetic, absorb(): new_sum = run_sum * factor + jnp.sum(weights, axis=-1)  78.2 us
    unnamed x3, waiting for transfers between devices  52.9 us
    squeeze x16, local copies, waits for them, and re-layouts, absorb_frame(): keys = kv_frame[0].reshape(span_rows * width, heads_dev, HD)  42.2 us
    another operation x1, loops' own time, body(): lax.scan(one_frame, empty_state(heads_dev, qcount), jnp.arange(piece.shap...  30.9 us
    slice x16, local copies, waits for them, and re-layouts, absorb_frame(): values = kv_frame[1].reshape(span_rows * width, heads_dev, HD)  30 us
  transfers between devices with their start and end apart: 4, of which 3 were waited for; matrix products, arithmetic and copies ran while one was open for 0% of the time, Pallas kernels for 0%

commit v1 on v0

--- a/solution.py
+++ b/solution.py
@@ -82,7 +82,12 @@
     key_rows = first_row - HALO + jnp.arange(rows_dev + 2 * HALO, dtype=jnp.int32)
     my_windows = lax.dynamic_slice_in_dim(window, first_frame, frames_dev, 0)
     queries = query.reshape(qcount, heads_dev, HD)
-    piece = lax.all_gather(padded, "tm", axis=1, tiled=True)
+    piece = jnp.concatenate(
+        jax.lax.all_to_all(
+            jnp.stack([padded for _ in range(jax.lax.psum(1, "tm"))], 0), "tm", 0, 0
+        ),
+        1,
+    )
 
     def one_frame(carry, offset):
         kv_frame = lax.dynamic_index_in_dim(piece, offset, 1, False)

time: 813 us -> 1190 us (1.46)
  waiting for transfers between devices: 286 us -> 641 us
  local copies, waits for them, and re-layouts: 141 us -> 158 us
    all_to_all x0 -> x1, waiting for transfers between devices: none -> 588 us  [body(): jax.lax.all_to_all(jnp.stack([padded for _ in range(jax.lax.psum(1, 'tm')...]
    all_gather x1 -> x0, waiting for transfers between devices: 231 us -> none  [body(): piece = lax.all_gather(padded, 'tm', axis=1, tiled=True)]
    dynamic_slice x0 -> x16, local copies, waits for them, and re-layouts: none -> 30.6 us  [one_frame(): kv_frame = lax.dynamic_index_in_dim(piece, offset, 1, False)]
    slice x16, local copies, waits for them, and re-layouts: 30 us -> 3.41 us  [absorb_frame(): values = kv_frame[1].reshape(span_rows * width, heads_dev, HD)]
    another operation x0 -> x1, local copies, waits for them, and re-layouts: none -> 13 us  [body(): jnp.stack([padded for _ in range(jax.lax.psum(1, 'tm'))], 0)]
    unnamed x3 -> x2, waiting for transfers between devices: 52.9 us -> 50.5 us
where the time goes in v1:
time: 1190 us
  waiting for transfers between devices  641 us (54%)
  matrix products  188 us (16%)
  local copies, waits for them, and re-layouts  158 us (13%)
  other arithmetic  143 us (12%)
  loops' own time  28.8 us (2%)
  between operations  13.5 us (1%)
  starting transfers between devices  12.8 us (1%)
    all_to_all x1, waiting for transfers between devices, body(): jax.lax.all_to_all(jnp.stack([padded for _ in range(jax.lax.psum(1, 'tm')...  588 us
    dot_general x16, matrix products, absorb(): jnp.einsum('qhd,khd->hqk', queries, keys, preferred_element_type=jnp.floa...  91.7 us
    dot_general x16, matrix products, absorb(): jnp.einsum('hqk,khd->hqd', weights.astype(jnp.bfloat16), values, preferre...  90.8 us
    reduce_sum x16, other arithmetic, absorb(): new_sum = run_sum * factor + jnp.sum(weights, axis=-1)  78.2 us
    unnamed x2, waiting for transfers between devices  50.5 us
    squeeze x16, local copies, waits for them, and re-layouts, absorb_frame(): keys = kv_frame[0].reshape(span_rows * width, heads_dev, HD)  42.7 us
    dynamic_slice x16, local copies, waits for them, and re-layouts, one_frame(): kv_frame = lax.dynamic_index_in_dim(piece, offset, 1, False)  30.6 us
    another operation x1, loops' own time, body(): lax.scan(one_frame, empty_state(heads_dev, qcount), jnp.arange(piece.shap...  28.8 us
  transfers between devices with their start and end apart: 4, of which 3 were waited for; matrix products, arithmetic and copies ran while one was open for 0% of the time, Pallas kernels for 0%

profile of v1, /device:TPU:1, one launch (start us, length us, event | category | flops | bytes accessed | tf_op | source)
XLA Modules:
  0.0 1185.1 jit_solution(3922289781178634507)
XLA Ops:
  9.1 5.2 collective-permute-start.1
  17.6 13.0 %stack.11 = bf16[16,2,1,12,80,640]{5,4,3,1,2,0:T(8,128)(2,1)} broadcast(bf16[2,12,80,640]{3,2,1,0:T(8,128)(2,1)S(1)} %maximum_bitcast_fusion), dimensions={1,3,4,5} | broadcast | bytes 41779200 | tf_op jit(solution)/shard_map/stack | solution.py:87
  30.6 6.3 all-to-all-start
  38.8 588.4 %all-to-all-done = bf16[16,2,1,12,80,640]{5,4,3,1,2,0:T(8,128)(2,1)} async-done(((bf16[16,2,1,12,80,640]{5,4,3,1,2,0:T(8,128)(2,1)}), bf16[16,2,1,12,80,640]{5,4,3,1,2,0:T(8,128)(2,1)}, u32[]{:S(2)}, u32[]{:S(2)}) %all-to-all-start) | async-done | bytes 39321632 | tf_op jit(solution)/shard_map/all_to_all | solution.py:86
  627.3 486.7 %while.15 = (s32[]{:T(128)}, f32[5,320]{1,0:T(8,128)S(1)}, f32[5,320]{1,0:T(8,128)}, f32[5,320,128]{2,1,0:T(8,128)}, s32[16]{0:T(128)S(1)}, /*index=5*/s32[1,16]...) while((s32[]{:T(128)}, f32[5,320]{1,0:T(8,128)S(1)}, ...), condition=%wide.region_3.4_spmd.clone, body=%wide.region_0.3_spmd.clone.sunk | while | flops 803950720 | bytes 40244324 | solution.py:100
  636.0 2.7 squeeze.19
  638.6 5.7 fusion.46
  644.4 4.9 fusion.47
  651.3 5.5 fusion.49
  665.6 2.7 squeeze.19
  668.2 5.7 fusion.46
  674.0 4.9 fusion.47
  681.6 5.7 fusion.49
  696.1 2.7 squeeze.19
  698.7 5.7 fusion.46
  704.5 4.9 fusion.47
  712.1 5.7 fusion.49
  726.5 2.7 squeeze.19
  729.2 5.7 fusion.46
  734.9 4.9 fusion.47
  742.6 5.7 fusion.49
  757.0 2.7 squeeze.19
  759.7 5.7 fusion.46
  765.4 4.9 fusion.47
  773.1 5.7 fusion.49
  787.5 2.7 squeeze.19
  790.1 5.7 fusion.46
  795.9 4.9 fusion.47
  803.5 5.7 fusion.49
  820.6 5.7 fusion.46
  826.3 4.9 fusion.47
  834.0 5.7 fusion.49
  851.1 5.7 fusion.46
  856.8 4.9 fusion.47
  864.5 5.7 fusion.49
  881.6 5.7 fusion.46
  887.3 4.9 fusion.47
  894.9 5.7 fusion.49
  912.0 5.7 fusion.46
  917.8 4.9 fusion.47
  925.4 5.7 fusion.49
  939.8 2.7 squeeze.19
  942.5 5.7 fusion.46
  948.2 4.9 fusion.47
  955.9 5.7 fusion.49
  970.3 2.7 squeeze.19
  973.0 5.7 fusion.46
  978.7 4.9 fusion.47
  986.4 5.7 fusion.49
  1003.4 5.7 fusion.46
  1009.2 4.9 fusion.47
  1016.8 5.7 fusion.49
  1033.9 5.7 fusion.46
  1039.6 4.9 fusion.47
  1047.3 5.7 fusion.49
  1064.4 5.7 fusion.46
  1070.1 4.9 fusion.47
  1077.8 5.7 fusion.49
  1094.9 5.7 fusion.46
  1100.6 4.9 fusion.47
  1108.3 5.7 fusion.49
  1116.4 5.8 fusion.23
  1122.2 3.6 copy.24
  1125.8 50.5 %reduce-scatter.4.cloned.1.call-done = bf16[640,320]{1,0:T(8,128)(2,1)} async-done(((bf16[5120,320]{1,0:T(8,128)(2,1)}), bf16[640,320]{1,0:T(8,128)(2,1)}) %reduce-scatter.4.cloned.1.call-update) | async-done | bytes 409616
  (351 shorter events, 188.0 us)
Async XLA Ops:
  6.5 31.8 %copy-start = (s32[16,16]{1,0:T(8,128)S(1)}, s32[16,16]{1,0:T(8,128)}, u32[]{:S(2)}) copy-start(s32[16,16]{1,0:T(8,128)} %param.10) | copy-start | bytes 3076
  7.8 6.5 collective-permute-start
  9.1 7.1 collective-permute-start.1
  30.6 6.4 copy-start.2
  30.6 596.7 %all-to-all-start = ((bf16[16,2,1,12,80,640]{5,4,3,1,2,0:T(8,128)(2,1)}), bf16[16,2,1,12,80,640]{5,4,3,1,2,0:T(8,128)(2,1)}, u32[]{:S(2)}, u32[]{:S(2)}) async-start(bf16[16,2,1,12,80,640]{5,4,3,1,2,0:T(8,128)(2,1)} %stack.11), calls=%async_computation | async-start | bytes 78643200 | tf_op jit(solution)/shard_map/all_to_all | solution.py:86
  36.9 1139.4 %reduce-scatter.4.cloned.1.call-start = ((), (), s32[]{:S(2)}) async-start(), calls=%async_computation.2 | async-start | bytes 4423680
  627.3 3.5 copy-start.3
  651.3 5.5 copy-start.4
  656.9 3.5 copy-start.3
  681.6 5.7 copy-start.4
  687.3 3.5 copy-start.3
  712.1 5.7 copy-start.4
  717.8 3.5 copy-start.3
  742.6 5.7 copy-start.4
  748.3 3.5 copy-start.3
  773.1 5.7 copy-start.4
  778.8 3.5 copy-start.3
  803.5 5.7 copy-start.4
  809.2 3.5 copy-start.3
  834.0 5.7 copy-start.4
  839.7 3.5 copy-start.3
  864.5 5.7 copy-start.4
  870.2 3.5 copy-start.3
  894.9 5.7 copy-start.4
  900.6 3.5 copy-start.3
  925.4 5.7 copy-start.4
  931.1 3.5 copy-start.3
  955.9 5.7 copy-start.4
  961.6 3.5 copy-start.3
  986.4 5.7 copy-start.4
  992.1 3.5 copy-start.3
  1016.8 5.7 copy-start.4
  1022.5 3.5 copy-start.3
  1047.3 5.7 copy-start.4
  1053.0 3.5 copy-start.3
  1077.8 5.7 copy-start.4
  1083.5 3.5 copy-start.3
  1108.2 5.7 copy-start.4
  1122.2 56.1 %copy-start.1 = (s32[16,16]{1,0:T(8,128)S(1)}, s32[16,16]{1,0:T(8,128)}, u32[]{:S(2)}) copy-start(s32[16,16]{1,0:T(8,128)} %param.10) | copy-start | bytes 3076
Sparse Core Ops, SparseCore 0:
  1126.0 50.2 reduce-scatter.3
